TPU v7x, 256 devices: a whole 4x4x8 slice. The times are simulated.
256 devices in a mesh: row: 32 (over x, z), col: 8 (over y, core).
Axes of the slice: x: 4, y: 4, z: 8, core: 2. Of those that a mesh axis runs over, the one named last changes fastest.
Arguments:
- tensor: bfloat16 [64, 2048, 2048], P(None, 'row', 'col'), may hold values from -6 to 6
- pattern: int32 [32, 32], P('col', 'row'), may hold values 0 or 1
- coef: bfloat16 [2048, 2048], P('row', 'col'), may hold values from -0.1875 to 0.1875
Outputs:
- contracted: bfloat16 [64, 2048, 2048], P(None, 'row', 'col')
All inputs are finite; a program needn't handle non-finite values. No bound on the sum of `pattern` on one device may be relied on, other than what follows from the above.
Results may differ from a plain program's by a relative error of at most 0.001.
Values may be sent and summed in bfloat16 or wider, within the bound.
A program may use at most 64 MiB of HBM per device.

v0:
```python
import jax
import jax.numpy as jnp
from jax import lax
from jax.sharding import PartitionSpec as P


def per_device(tensor, pattern, coef):
    mu_all, nu_loc, aux_loc = tensor.shape
    atoms_aux, atoms_nu = pattern.shape
    blk = aux_loc // atoms_aux
    keep = jnp.transpose(pattern).astype(jnp.bfloat16)[None, :, None, :, None]
    masked = (tensor.reshape(mu_all, atoms_nu, blk, atoms_aux, blk) * keep).reshape(
        mu_all, nu_loc, aux_loc
    )
    matrix = lax.all_to_all(masked, "row", split_axis=0, concat_axis=1, tiled=True)
    form = "mna,no->moa"
    panel = lax.all_gather(coef, "col", axis=1, tiled=True)
    whole = lax.all_gather(panel, "row", axis=0, tiled=True)
    product = jnp.einsum(form, matrix, whole, preferred_element_type=jnp.float32)
    result = product.astype(jnp.bfloat16)
    return lax.all_to_all(result, "row", split_axis=1, concat_axis=0, tiled=True)


def solution(mesh):
    return jax.shard_map(
        per_device,
        mesh=mesh,
        in_specs=(P(None, "row", "col"), P("col", "row"), P("row", "col")),
        out_specs=P(None, "row", "col"),
        check_vma=False,
    )
```

profile of v0, /device:TPU:1, one launch (start us, length us, event | category | flops | bytes accessed | tf_op | source)
XLA Modules:
  0.0 213.9 jit_solution(12455503580650013508)
XLA Ops:
  6.5 0.0 all-gather.2.cloned.1.call-start
  6.5 17.3 %all_gather.6 = bf16[64,2048]{1,0:T(8,128)(2,1)} all-gather(bf16[64,256]{1,0:T(8,128)(2,1)} %param.5), channel_id=1, replica_groups=mesh['row'=32,'col'=8] {'col'}, dimensions={1}, use_global_device_ids=true | all-gather | bytes 294912 | tf_op jit(solution)/shard_map/all_gather | solution.py:17
  23.8 0.0 all-gather.2.cloned.1.call-update
  23.8 0.7 convert_bitcast_fusion
  24.5 0.1 mul.15
  24.6 0.1 mul.16
  24.7 1.7 broadcast_multiply_fusion
  26.4 67.3 %all_to_all.36 = bf16[64,64,256]{2,1,0:T(8,128)(2,1)S(1)} all-to-all(bf16[64,64,256]{2,1,0:T(8,128)(2,1)S(1)} %broadcast_multiply_fusion), channel_id=1, replica_groups=mesh['row'=32,'col'=8] {'row'}, dimensions={0} | all-to-all | bytes 4194304 | tf_op jit(solution)/shard_map/all_to_all | solution.py:15
  93.7 0.1 copy.12
  93.8 44.7 %all-gather.2.cloned.1.call-done = bf16[2048,2048]{1,0:T(8,128)(2,1)} async-done(((bf16[64,2048]{1,0:T(8,128)(2,1)}), bf16[2048,2048]{1,0:T(8,128)(2,1)}) %all-gather.2.cloned.1.call-update) | async-done | bytes 8388624 | tf_op jit(solution)/shard_map/all_gather | solution.py:18
  138.5 9.1 %fusion.5 = bf16[2,2048,256]{1,2,0:T(8,128)(2,1)} fusion(bf16[2,2048,256]{2,1,0:T(8,128)(2,1)S(1)} %bitcast.22, bf16[2048,2048]{1,0:T(8,128)(2,1)} %all-gather.2.cloned.1.call-done), kind=kOutput, calls=%fused_computation.3 | convolution fusion | flops 4296015872 | bytes 12582912 | tf_op jit(solution)/shard_map/mna,no->moa/dot_general | solution.py:19
  147.6 4.8 %copy.14 = bf16[2,2048,256]{2,0,1:T(2,128)(2,1)S(1)} copy(bf16[2,2048,256]{1,2,0:T(8,128)(2,1)} %fusion.5) | data formatting | bytes 4194304 | tf_op jit(solution)/shard_map/convert_element_type | solution.py:20
  152.4 52.9 %all_to_all.37 = bf16[2,2048,256]{2,0,1:T(2,128)(2,1)S(1)} all-to-all(bf16[2,2048,256]{2,0,1:T(2,128)(2,1)S(1)} %copy.14), channel_id=1, replica_groups=mesh['row'=32,'col'=8] {'row'}, dimensions={1} | all-to-all | bytes 4194304 | tf_op jit(solution)/shard_map/all_to_all | solution.py:21
  205.3 0.3 copy.15
  205.6 1.5 copy.16
Async XLA Ops:
  6.5 132.0 %all-gather.2.cloned.1.call-start = ((), (), s32[]{:S(2)}) async-start(), calls=%async_computation.2 | async-start | bytes 8650752 | tf_op jit(solution)/shard_map/all_gather | solution.py:18
Sparse Core Ops, SparseCore 0:
  24.0 114.4 all-gather.1
where the time goes:
time: 218 us; the launch traced here: 214 us
  blocking collectives  137 us (63%)
  waiting for transfers between devices  44.7 us (21%)
  between operations  13.4 us (6%)
  matrix products  9.1 us (4%)
  local copies, waits for them, and re-layouts  6.85 us (3%)
  other arithmetic  2.39 us (1%)
    all_to_all x1, blocking collectives, per_device(): lax.all_to_all(masked, 'row', split_axis=0, concat_axis=1, tiled=True)  67.3 us
    all_to_all x1, blocking collectives, per_device(): lax.all_to_all(result, 'row', split_axis=1, concat_axis=0, tiled=True)  52.9 us
    all_gather x1, waiting for transfers between devices, per_device(): whole = lax.all_gather(panel, 'row', axis=0, tiled=True)  44.7 us
    all_gather x1, blocking collectives, per_device(): panel = lax.all_gather(coef, 'col', axis=1, tiled=True)  17.3 us
    dot_general x1, matrix products, per_device(): jnp.einsum(form, matrix, whole, preferred_element_type=jnp.float32)  9.1 us
    convert_element_type x1, local copies, waits for them, and re-layouts, per_device(): result = product.astype(jnp.bfloat16)  4.82 us
  transfers between devices with their start and end apart: 1, of which 1 were waited for; matrix products, arithmetic and copies ran while one was open for 1% of the time, Pallas kernels for 0%

commit v1 on v0

v1 whole, which is shorter than its diff:
```python
import jax
import jax.numpy as jnp
from jax import lax
from jax.experimental import pallas as pl
from jax.experimental.pallas import tpu as pltpu
from jax.sharding import PartitionSpec as P

MESH = pl.DeviceIdType.MESH
X, Y, Z, CORES = 4, 4, 8, 2
ROWS, COLS = X * Z, Y * CORES


def kernel(
    pattern, tensor, coef, out,
    raw, masked, matrix, whole, result,
    load_sem, own_sem, send_sem, matrix_sem, out_sem,
    coef_send, z_sem, x_sem, y_sem, relay_sem, core_sem,
):
    atoms, blk = pattern.shape[0], tensor.shape[2] // pattern.shape[0]
    mu_all, nu_loc, aux_loc = tensor.shape
    mu_per = mu_all // ROWS
    row, col = lax.axis_index("row"), lax.axis_index("col")
    x, z = row // Z, lax.rem(row, Z)
    y, core = col // CORES, lax.rem(col, CORES)

    def at(dx, dz):
        return lax.rem(x + dx, X) * Z + lax.rem(z + dz, Z)

    def col_at(dy):
        return lax.rem(y + dy, Y) * CORES + core

    partner = y * CORES + (1 - core)

    loads = []
    step = mu_all // 4
    for q in range(4):
        part = pl.ds(q * step, step)
        load = pltpu.make_async_copy(tensor.at[part], raw.at[part], load_sem.at[q])
        load.start()
        loads.append(load)
    n_rows = pl.ds(pl.multiple_of(row * nu_loc, nu_loc), nu_loc)
    own_coef = pltpu.make_async_copy(coef, whole.at[col, n_rows], load_sem.at[4])
    own_coef.start()

    barrier = pltpu.get_barrier_semaphore()

    def greet(k, carry):
        pl.semaphore_signal(
            barrier, 1, device_id={"row": at(k // Z, lax.rem(k, Z))}, device_id_type=MESH
        )
        return carry

    lax.fori_loop(1, ROWS, greet, 0)
    for dy in range(1, Y):
        pl.semaphore_signal(barrier, 1, device_id={"col": col_at(dy)}, device_id_type=MESH)
    pl.semaphore_signal(barrier, 1, device_id={"col": partner}, device_id_type=MESH)

    lane = lax.broadcasted_iota(jnp.int32, (1, 1, aux_loc), 2)
    keep = jnp.zeros((1, 1, aux_loc), jnp.float32)
    for a in range(atoms):
        here = (lane >= a * blk) & (lane < (a + 1) * blk)
        keep = jnp.where(here, pattern[a, 0].astype(jnp.float32), keep)
    keep = keep.astype(jnp.bfloat16)
    for q in range(4):
        loads[q].wait()

        def mask(i, carry):
            some = pl.ds(q * step + i * 2, 2)
            masked[some] = raw[some] * keep
            return carry

        lax.fori_loop(0, step // 2, mask, 0)
    own_coef.wait()
    pl.semaphore_wait(barrier, ROWS - 1 + Y - 1 + 1)

    def send_coef(stage, rows, which, sem, **device):
        block = whole.at[which, rows]
        copy = pltpu.make_async_remote_copy(
            block, block, coef_send.at[stage], sem, device_id=device, device_id_type=MESH
        )
        copy.start()

    for dz in range(1, Z):
        send_coef(0, n_rows, col, z_sem, row=at(0, dz))

    for m in range(mu_per):

        def send_block(k, carry):
            peer = at(k // Z, lax.rem(k, Z))
            pltpu.make_async_remote_copy(
                masked.at[peer * mu_per + m], matrix.at[m, n_rows], send_sem.at[0],
                matrix_sem.at[m], device_id={"row": peer}, device_id_type=MESH,
            ).start()
            return carry

        lax.fori_loop(1, ROWS, send_block, 0)
        pltpu.make_async_copy(
            masked.at[row * mu_per + m], matrix.at[m, n_rows], own_sem.at[m]
        ).start()

    slab = Z * nu_loc

    def x_rows(dx):
        return pl.ds(pl.multiple_of(lax.rem(x + dx, X) * slab, slab), slab)

    def wait_rows(count, sem):
        block = whole.at[0, pl.ds(0, count)]
        pltpu.make_async_copy(block, block, sem).wait()

    def spread(dx):
        rows = x_rows(dx)
        send_coef(2, rows, col, y_sem.at[0, dx], col=col_at(1))
        send_coef(2, rows, col, y_sem.at[1, dx], col=col_at(Y - 1))
        send_coef(4, rows, col, core_sem, col=partner)

    wait_rows((Z - 1) * nu_loc, z_sem)
    for dx in (1, 3, 2):
        send_coef(1, x_rows(0), col, x_sem.at[dx - 1], row=at(dx, 0))
    spread(0)
    for s in (1, 3, 2):
        wait_rows(slab, x_sem.at[s - 1])
        spread(X - s)
    for i, dx in enumerate((0, 3, 1, 2)):
        rows = x_rows(dx)
        wait_rows(slab, y_sem.at[0, dx])
        if i < 2:
            send_coef(3, rows, col_at(Y - 1), relay_sem.at[0, i], col=col_at(1))
        send_coef(4, rows, col_at(Y - 1), core_sem, col=partner)
        wait_rows(slab, y_sem.at[1, dx])
        if i >= 2:
            send_coef(3, rows, col_at(1), relay_sem.at[1, i - 2], col=col_at(Y - 1))
        send_coef(4, rows, col_at(1), core_sem, col=partner)
    for i, dx in enumerate((0, 3, 1, 2)):
        wait_rows(slab, relay_sem.at[i // 2, i % 2])
        send_coef(4, x_rows(dx), col_at(2), core_sem, col=partner)
    half = whole.at[pl.ds(0, Y)]
    pltpu.make_async_copy(half, half, core_sem).wait()

    for m in range(mu_per):
        own = pltpu.make_async_copy(
            masked.at[row * mu_per + m], matrix.at[m, n_rows], own_sem.at[m]
        )
        own.wait()
        most = matrix.at[m, pl.ds(0, (ROWS - 1) * nu_loc)]
        pltpu.make_async_copy(most, most, matrix_sem.at[m]).wait()
        per = aux_loc // nu_loc

        def tile(k, carry):
            t = lax.rem(row // per + k, COLS)
            product = lax.dot_general(
                whole[t], matrix[m], (((0,), (0,)), ((), ())),
                preferred_element_type=jnp.float32,
            )
            result[m, pl.ds(pl.multiple_of(t * aux_loc, aux_loc), aux_loc)] = product.astype(
                jnp.bfloat16
            )
            for j in range(per):
                peer = t * per + j

                @pl.when(peer != row)
                def _():
                    pltpu.make_async_remote_copy(
                        result.at[m, pl.ds(pl.multiple_of(peer * nu_loc, nu_loc), nu_loc)],
                        out.at[row * mu_per + m], send_sem.at[1], out_sem,
                        device_id={"row": peer}, device_id_type=MESH,
                    ).start()

            return carry

        lax.fori_loop(0, COLS, tile, 0)
        pltpu.make_async_copy(
            result.at[m, n_rows], out.at[row * mu_per + m], own_sem.at[m]
        ).start()

    for m in range(mu_per):
        pltpu.make_async_copy(
            result.at[m, n_rows], out.at[row * mu_per + m], own_sem.at[m]
        ).wait()
    most = masked.at[pl.ds(0, (ROWS - 1) * mu_per)]
    pltpu.make_async_copy(most, most, out_sem).wait()
    pltpu.make_async_copy(most, most, send_sem.at[0]).wait()
    pltpu.make_async_copy(most, most, send_sem.at[1]).wait()
    wait_rows((Z - 1) * nu_loc, coef_send.at[0])
    wait_rows((X - 1) * slab, coef_send.at[1])
    quarter = whole.at[pl.ds(0, 2)]
    pltpu.make_async_copy(quarter, quarter, coef_send.at[2]).wait()
    wait_rows(X * slab, coef_send.at[3])
    pltpu.make_async_copy(half, half, coef_send.at[4]).wait()


def per_device(tensor, pattern, coef):
    mu_all, nu_loc, aux_loc = tensor.shape
    mu_per = mu_all // ROWS
    nu_all = nu_loc * ROWS
    dma = pltpu.SemaphoreType.DMA
    return pl.pallas_call(
        kernel,
        out_shape=jax.ShapeDtypeStruct(tensor.shape, jnp.bfloat16),
        in_specs=[
            pl.BlockSpec(memory_space=pltpu.SMEM),
            pl.BlockSpec(memory_space=pl.ANY),
            pl.BlockSpec(memory_space=pl.ANY),
        ],
        out_specs=pl.BlockSpec(memory_space=pl.ANY),
        scratch_shapes=[
            pltpu.VMEM(tensor.shape, jnp.bfloat16),
            pltpu.VMEM(tensor.shape, jnp.bfloat16),
            pltpu.VMEM((mu_per, nu_all, aux_loc), jnp.bfloat16),
            pltpu.VMEM((COLS, nu_all, aux_loc), jnp.bfloat16),
            pltpu.VMEM((mu_per, nu_all, aux_loc), jnp.bfloat16),
            dma((5,)), dma((mu_per,)), dma((2,)), dma((mu_per,)), dma(()),
            dma((5,)), dma(()), dma((X - 1,)), dma((2, X)), dma((2, 2)), dma(()),
        ],
        compiler_params=pltpu.CompilerParams(
            collective_id=0, has_side_effects=True, vmem_limit_bytes=40 * 1024 * 1024
        ),
    )(pattern, tensor, coef)


def solution(mesh):
    return jax.shard_map(
        per_device,
        mesh=mesh,
        in_specs=(P(None, "row", "col"), P("col", "row"), P("row", "col")),
        out_specs=P(None, "row", "col"),
        check_vma=False,
    )
```

time: 218 us -> 120 us (0.55); the launches traced: 214 us -> 120 us
  blocking collectives: 137 us -> 0 us
  Pallas kernels: 0 us -> 116 us
  waiting for transfers between devices: 44.7 us -> 0 us
  between operations: 13.4 us -> 0.01 us
  matrix products: 9.1 us -> 0 us
  local copies, waits for them, and re-layouts: 6.85 us -> 4.41 us
  other arithmetic: 2.39 us -> 0 us
    all_to_all x2 -> x0, blocking collectives: 120 us -> none  [the longest x1 67.3 us: per_device(): lax.all_to_all(masked, 'row', split_axis=0, concat_axis=1, tiled=True)]
    pallas_call x0 -> x1, Pallas kernels: none -> 116 us  [per_device(): pl.pallas_call(kernel, out_shape=jax.ShapeDtypeStruct(tensor.shape, jnp.b...]
    all_gather x1 -> x0, waiting for transfers between devices: 44.7 us -> none  [per_device(): whole = lax.all_gather(panel, 'row', axis=0, tiled=True)]
    all_gather x1 -> x0, blocking collectives: 17.3 us -> none  [per_device(): panel = lax.all_gather(coef, 'col', axis=1, tiled=True)]
    dot_general x1 -> x0, matrix products: 9.1 us -> none  [per_device(): jnp.einsum(form, matrix, whole, preferred_element_type=jnp.float32)]
    convert_element_type x1 -> x0, local copies, waits for them, and re-layouts: 4.82 us -> none  [per_device(): result = product.astype(jnp.bfloat16)]
    unnamed x0 -> x6, local copies, waits for them, and re-layouts: none -> 4.41 us
  transfers between devices with their start and end apart: 1 -> 0, of which waited for: 1 -> 0; matrix products, arithmetic and copies ran while one was open for 1% -> 0% of each run, Pallas kernels for 0% -> 0%
where the time goes in v1:
time: 120 us
  Pallas kernels  116 us (97%)
  local copies, waits for them, and re-layouts  4.41 us (4%)
    pallas_call x1, Pallas kernels, per_device(): pl.pallas_call(kernel, out_shape=jax.ShapeDtypeStruct(tensor.shape, jnp.b...  116 us
    unnamed x6, local copies, waits for them, and re-layouts  4.41 us

profile of v1, /device:TPU:1, one launch (start us, length us, event | category | flops | bytes accessed | tf_op | source)
XLA Modules:
  0.0 120.0 jit_solution(11528292427222920143)
XLA Ops:
  0.0 0.7 copy.4.pattern
  0.7 0.0 copy-start
  0.7 1.6 %copy-done = bf16[64,64,256]{2,1,0:T(8,128)(2,1)S(1)} copy-done((bf16[64,64,256]{2,1,0:T(8,128)(2,1)S(1)}, bf16[64,64,256]{2,1,0:T(8,128)(2,1)}, u32[]{:S(2)}) %copy-start) | copy-done | bytes 2097176
  2.3 0.0 copy-start.1
  2.3 0.8 copy-done.1
  3.1 115.6 %shard_map.37 = bf16[64,64,256]{2,1,0:T(8,128)(2,1)S(1)} custom-call(s32[4,1]{1,0:T(4,128)S(1)} %copy.4.pattern, bf16[64,64,256]{2,1,0:T(8,128)(2,1)S(1)} %copy-done, bf16[64,256]{1,0:T(8,128)(2,1)S(1)} %copy-done.1), custom_call_target="tpu_custom_call" | custom-call | tf_op jit(solution)/shard_map/pallas_call | solution.py:196
  118.7 1.3 %copy.6 = bf16[64,64,256]{2,1,0:T(8,128)(2,1)} copy(bf16[64,64,256]{2,1,0:T(8,128)(2,1)S(1)} %shard_map.37) | data formatting | bytes 4194304
Async XLA Ops:
  0.7 1.6 %copy-start = (bf16[64,64,256]{2,1,0:T(8,128)(2,1)S(1)}, bf16[64,64,256]{2,1,0:T(8,128)(2,1)}, u32[]{:S(2)}) copy-start(bf16[64,64,256]{2,1,0:T(8,128)(2,1)} %tensor.1) | copy-start | bytes 6291460
  2.3 0.8 copy-start.1

commit v2 on v1

--- a/solution.py
+++ b/solution.py
@@ -8,15 +8,17 @@
 MESH = pl.DeviceIdType.MESH
 X, Y, Z, CORES = 4, 4, 8, 2
 ROWS, COLS = X * Z, Y * CORES
+SPLIT = 6
 
 
 def kernel(
-    pattern, tensor, coef, out,
-    raw, masked, matrix, whole, result,
+    pattern_hbm, tensor, coef, out,
+    pattern, raw, masked, matrix, whole, result,
     load_sem, own_sem, send_sem, matrix_sem, out_sem,
     coef_send, z_sem, x_sem, y_sem, relay_sem, core_sem,
 ):
-    atoms, blk = pattern.shape[0], tensor.shape[2] // pattern.shape[0]
+    atoms = pattern.shape[1]
+    blk = tensor.shape[2] // atoms
     mu_all, nu_loc, aux_loc = tensor.shape
     mu_per = mu_all // ROWS
     row, col = lax.axis_index("row"), lax.axis_index("col")
@@ -31,6 +33,11 @@
 
     partner = y * CORES + (1 - core)
 
+    own_pattern = pltpu.make_async_copy(pattern_hbm, pattern, load_sem.at[5])
+    own_pattern.start()
+    n_rows = pl.ds(pl.multiple_of(row * nu_loc, nu_loc), nu_loc)
+    own_coef = pltpu.make_async_copy(coef, whole.at[col, n_rows], load_sem.at[4])
+    own_coef.start()
     loads = []
     step = mu_all // 4
     for q in range(4):
@@ -38,29 +45,24 @@
         load = pltpu.make_async_copy(tensor.at[part], raw.at[part], load_sem.at[q])
         load.start()
         loads.append(load)
-    n_rows = pl.ds(pl.multiple_of(row * nu_loc, nu_loc), nu_loc)
-    own_coef = pltpu.make_async_copy(coef, whole.at[col, n_rows], load_sem.at[4])
-    own_coef.start()
 
     barrier = pltpu.get_barrier_semaphore()
-
-    def greet(k, carry):
-        pl.semaphore_signal(
-            barrier, 1, device_id={"row": at(k // Z, lax.rem(k, Z))}, device_id_type=MESH
-        )
-        return carry
-
-    lax.fori_loop(1, ROWS, greet, 0)
+    hops = lambda d, n: min(d, n - d)
+    peers = [(dx, dz) for dx in range(X) for dz in range(Z) if dx or dz]
+    for dx, dz in sorted(peers, key=lambda o: -hops(o[0], X) - hops(o[1], Z)):
+        pl.semaphore_signal(barrier, 1, device_id={"row": at(dx, dz)}, device_id_type=MESH)
     for dy in range(1, Y):
         pl.semaphore_signal(barrier, 1, device_id={"col": col_at(dy)}, device_id_type=MESH)
     pl.semaphore_signal(barrier, 1, device_id={"col": partner}, device_id_type=MESH)
 
+    own_pattern.wait()
     lane = lax.broadcasted_iota(jnp.int32, (1, 1, aux_loc), 2)
     keep = jnp.zeros((1, 1, aux_loc), jnp.float32)
     for a in range(atoms):
         here = (lane >= a * blk) & (lane < (a + 1) * blk)
-        keep = jnp.where(here, pattern[a, 0].astype(jnp.float32), keep)
+        keep = jnp.where(here, pattern[0, a].astype(jnp.float32), keep)
     keep = keep.astype(jnp.bfloat16)
+    own_coef.wait()
     for q in range(4):
         loads[q].wait()
 
@@ -70,7 +72,6 @@
             return carry
 
         lax.fori_loop(0, step // 2, mask, 0)
-    own_coef.wait()
     pl.semaphore_wait(barrier, ROWS - 1 + Y - 1 + 1)
 
     def send_coef(stage, rows, which, sem, **device):
@@ -98,41 +99,74 @@
             masked.at[row * mu_per + m], matrix.at[m, n_rows], own_sem.at[m]
         ).start()
 
-    slab = Z * nu_loc
-
-    def x_rows(dx):
-        return pl.ds(pl.multiple_of(lax.rem(x + dx, X) * slab, slab), slab)
+    slab, first = Z * nu_loc, SPLIT * nu_loc
+    sizes = (first, slab - first)
+
+    def rows_of(g, dx):
+        start = lax.rem(x + dx, X) * slab + g * first
+        return pl.ds(pl.multiple_of(start, nu_loc), sizes[g])
 
     def wait_rows(count, sem):
         block = whole.at[0, pl.ds(0, count)]
         pltpu.make_async_copy(block, block, sem).wait()
 
-    def spread(dx):
-        rows = x_rows(dx)
-        send_coef(2, rows, col, y_sem.at[0, dx], col=col_at(1))
-        send_coef(2, rows, col, y_sem.at[1, dx], col=col_at(Y - 1))
-        send_coef(4, rows, col, core_sem, col=partner)
-
+    def one(g, d):
+        return (rows_of(0, d), col) if g == 0 else (rows_of(1, 0), col_at(d))
+
+    def both(g, d, e):
+        return (rows_of(0, d), col_at(e)) if g == 0 else (rows_of(1, e), col_at(d))
+
+    def first_to(g, d):
+        return {"row": at(d, 0)} if g == 0 else {"col": col_at(d)}
+
+    def second_to(g, d):
+        return {"col": col_at(d)} if g == 0 else {"row": at(d, 0)}
+
+    def spread(g, d):
+        rows, which = one(g, d)
+        send_coef(2, rows, which, y_sem.at[g, 0, d], **second_to(g, 1))
+        send_coef(2, rows, which, y_sem.at[g, 1, d], **second_to(g, 3))
+        send_coef(4, rows, which, core_sem, col=partner)
+
+    def arrive_first(g, s):
+        wait_rows(sizes[g], x_sem.at[g, s - 1])
+        spread(g, X - s)
+
+    def arrive_second(g, i, d):
+        rows, which = both(g, d, 3)
+        wait_rows(sizes[g], y_sem.at[g, 0, d])
+        if i < 2:
+            send_coef(3, rows, which, relay_sem.at[g, i], **second_to(g, 1))
+        send_coef(4, rows, which, core_sem, col=partner)
+        rows, which = both(g, d, 1)
+        wait_rows(sizes[g], y_sem.at[g, 1, d])
+        if i >= 2:
+            send_coef(3, rows, which, relay_sem.at[g, i], **second_to(g, 3))
+        send_coef(4, rows, which, core_sem, col=partner)
+
+    def arrive_relay(g, i, d):
+        rows, which = both(g, d, 2)
+        wait_rows(sizes[g], relay_sem.at[g, i])
+        send_coef(4, rows, which, core_sem, col=partner)
+
+    order = (0, 3, 1, 2)
+    groups = [g for g in range(2) if sizes[g]]
     wait_rows((Z - 1) * nu_loc, z_sem)
-    for dx in (1, 3, 2):
-        send_coef(1, x_rows(0), col, x_sem.at[dx - 1], row=at(dx, 0))
-    spread(0)
     for s in (1, 3, 2):
-        wait_rows(slab, x_sem.at[s - 1])
-        spread(X - s)
-    for i, dx in enumerate((0, 3, 1, 2)):
-        rows = x_rows(dx)
-        wait_rows(slab, y_sem.at[0, dx])
-        if i < 2:
-            send_coef(3, rows, col_at(Y - 1), relay_sem.at[0, i], col=col_at(1))
-        send_coef(4, rows, col_at(Y - 1), core_sem, col=partner)
-        wait_rows(slab, y_sem.at[1, dx])
-        if i >= 2:
-            send_coef(3, rows, col_at(1), relay_sem.at[1, i - 2], col=col_at(Y - 1))
-        send_coef(4, rows, col_at(1), core_sem, col=partner)
-    for i, dx in enumerate((0, 3, 1, 2)):
-        wait_rows(slab, relay_sem.at[i // 2, i % 2])
-        send_coef(4, x_rows(dx), col_at(2), core_sem, col=partner)
+        for g in groups:
+            rows, which = one(g, 0)
+            send_coef(1, rows, which, x_sem.at[g, s - 1], **first_to(g, s))
+    for g in groups:
+        spread(g, 0)
+    for s in (1, 3, 2):
+        for g in groups[::-1]:
+            arrive_first(g, s)
+    for i, d in enumerate(order):
+        for g in groups:
+            arrive_second(g, i, d)
+    for i, d in enumerate(order):
+        for g in groups:
+            arrive_relay(g, i, d)
     half = whole.at[pl.ds(0, Y)]
     pltpu.make_async_copy(half, half, core_sem).wait()
 
@@ -190,6 +224,9 @@
 
 def per_device(tensor, pattern, coef):
     mu_all, nu_loc, aux_loc = tensor.shape
+    inputs = [
+        pltpu.with_memory_space_constraint(v, pltpu.HBM) for v in (pattern.T, tensor, coef)
+    ]
     mu_per = mu_all // ROWS
     nu_all = nu_loc * ROWS
     dma = pltpu.SemaphoreType.DMA
@@ -197,24 +234,25 @@
         kernel,
         out_shape=jax.ShapeDtypeStruct(tensor.shape, jnp.bfloat16),
         in_specs=[
-            pl.BlockSpec(memory_space=pltpu.SMEM),
-            pl.BlockSpec(memory_space=pl.ANY),
-            pl.BlockSpec(memory_space=pl.ANY),
+            pl.BlockSpec(memory_space=pltpu.HBM),
+            pl.BlockSpec(memory_space=pltpu.HBM),
+            pl.BlockSpec(memory_space=pltpu.HBM),
         ],
         out_specs=pl.BlockSpec(memory_space=pl.ANY),
         scratch_shapes=[
+            pltpu.SMEM((1, pattern.shape[0]), jnp.int32),
             pltpu.VMEM(tensor.shape, jnp.bfloat16),
             pltpu.VMEM(tensor.shape, jnp.bfloat16),
             pltpu.VMEM((mu_per, nu_all, aux_loc), jnp.bfloat16),
             pltpu.VMEM((COLS, nu_all, aux_loc), jnp.bfloat16),
             pltpu.VMEM((mu_per, nu_all, aux_loc), jnp.bfloat16),
-            dma((5,)), dma((mu_per,)), dma((2,)), dma((mu_per,)), dma(()),
-            dma((5,)), dma(()), dma((X - 1,)), dma((2, X)), dma((2, 2)), dma(()),
+            dma((6,)), dma((mu_per,)), dma((2,)), dma((mu_per,)), dma(()),
+            dma((5,)), dma(()), dma((2, 3)), dma((2, 2, 4)), dma((2, 4)), dma(()),
         ],
         compiler_params=pltpu.CompilerParams(
             collective_id=0, has_side_effects=True, vmem_limit_bytes=40 * 1024 * 1024
         ),
-    )(pattern, tensor, coef)
+    )(*inputs)
 
 
 def solution(mesh):

time: 120 us -> 110 us (0.917)
  Pallas kernels: 116 us -> 108 us
  local copies, waits for them, and re-layouts: 4.41 us -> 1.32 us
    pallas_call x1, Pallas kernels: 116 us -> 108 us  [per_device(): pl.pallas_call(kernel, out_shape=jax.ShapeDtypeStruct(tensor.shape, jnp.b...]
    unnamed x6 -> x1, local copies, waits for them, and re-layouts: 4.41 us -> 1.32 us
where the time goes in v2:
time: 110 us
  Pallas kernels  108 us (98%)
  local copies, waits for them, and re-layouts  1.32 us (1%)
    pallas_call x1, Pallas kernels, per_device(): pl.pallas_call(kernel, out_shape=jax.ShapeDtypeStruct(tensor.shape, jnp.b...  108 us

profile of v2, /device:TPU:1, one launch (start us, length us, event | category | flops | bytes accessed | tf_op | source)
XLA Modules:
  0.0 109.6 jit_solution(9354627200679297753)
XLA Ops:
  0.0 108.2 %shard_map.37 = bf16[64,64,256]{2,1,0:T(8,128)(2,1)S(1)} custom-call(s32[1,4]{1,0:T(1,128)} %bitcast.1, bf16[64,64,256]{2,1,0:T(8,128)(2,1)} %tensor.1, bf16[64,256]{1,0:T(8,128)(2,1)} %coef.1), custom_call_target="tpu_custom_call" | custom-call | tf_op jit(solution)/shard_map/pallas_call | solution.py:233
  108.2 1.3 %copy.5 = bf16[64,64,256]{2,1,0:T(8,128)(2,1)} copy(bf16[64,64,256]{2,1,0:T(8,128)(2,1)S(1)} %shard_map.37) | data formatting | bytes 4194304

commit v3 on v2

--- a/solution.py
+++ b/solution.py
@@ -1,3 +1,5 @@
+import functools
+
 import jax
 import jax.numpy as jnp
 from jax import lax
@@ -8,7 +10,9 @@
 MESH = pl.DeviceIdType.MESH
 X, Y, Z, CORES = 4, 4, 8, 2
 ROWS, COLS = X * Z, Y * CORES
-SPLIT = 6
+NEAR = 2
+SPLIT = 2 * NEAR + 1
+BATCH = 12
 
 
 def kernel(
@@ -36,7 +40,15 @@
     own_pattern = pltpu.make_async_copy(pattern_hbm, pattern, load_sem.at[5])
     own_pattern.start()
     n_rows = pl.ds(pl.multiple_of(row * nu_loc, nu_loc), nu_loc)
-    own_coef = pltpu.make_async_copy(coef, whole.at[col, n_rows], load_sem.at[4])
+    slab, first = Z * nu_loc, SPLIT * nu_loc
+
+    def z_rows(dz, half=None):
+        start = pl.multiple_of(x * slab + lax.rem(dz + NEAR + Z, Z) * nu_loc, nu_loc)
+        if half is None:
+            return pl.ds(start, nu_loc)
+        return pl.ds(pl.multiple_of(start + half * (nu_loc // 2), nu_loc // 2), nu_loc // 2)
+
+    own_coef = pltpu.make_async_copy(coef, whole.at[col, z_rows(0)], load_sem.at[4])
     own_coef.start()
     loads = []
     step = mu_all // 4
@@ -74,41 +86,54 @@
         lax.fori_loop(0, step // 2, mask, 0)
     pl.semaphore_wait(barrier, ROWS - 1 + Y - 1 + 1)
 
+    def send_rows(stage, which, rows, to_rows, sem, **device):
+        pltpu.make_async_remote_copy(
+            whole.at[which, rows], whole.at[which, to_rows], coef_send.at[stage], sem,
+            device_id=device, device_id_type=MESH,
+        ).start()
+
     def send_coef(stage, rows, which, sem, **device):
-        block = whole.at[which, rows]
-        copy = pltpu.make_async_remote_copy(
-            block, block, coef_send.at[stage], sem, device_id=device, device_id_type=MESH
+        send_rows(stage, which, rows, rows, sem, **device)
+
+    def wait_rows(count, sem):
+        block = whole.at[0, pl.ds(0, count)]
+        pltpu.make_async_copy(block, block, sem).wait()
+
+    for dz in (2, -2, 1, -1):
+        send_rows(
+            0, col, z_rows(0), z_rows(-dz), z_sem.at[2 + dz], row=at(0, (dz + Z) % Z)
         )
-        copy.start()
-
-    for dz in range(1, Z):
-        send_coef(0, n_rows, col, z_sem, row=at(0, dz))
-
+
+    def send_block(m, k, carry):
+        j = lax.rem(k * 27, ROWS)
+        dz = lax.rem(j, Z)
+        peer = at(j // Z, dz)
+        pltpu.make_async_remote_copy(
+            masked.at[peer * mu_per + m], matrix.at[m, z_rows(-dz)], send_sem.at[0],
+            matrix_sem.at[m], device_id={"row": peer}, device_id_type=MESH,
+        ).start()
+        return carry
+
+    lax.fori_loop(1, 1 + BATCH, functools.partial(send_block, 0), 0)
+
+    for s, half in ((2, 0), (-2, 1)):
+        wait_rows(nu_loc, z_sem.at[2 + s])
+        d = s // 2
+        send_rows(0, col, z_rows(-s), z_rows(-s - d), z_sem.at[5], row=at(0, d % Z))
+        send_rows(
+            0, col, z_rows(-s, half), z_rows(-2 * s, half), z_sem.at[5], row=at(0, s % Z)
+        )
     for m in range(mu_per):
-
-        def send_block(k, carry):
-            peer = at(k // Z, lax.rem(k, Z))
-            pltpu.make_async_remote_copy(
-                masked.at[peer * mu_per + m], matrix.at[m, n_rows], send_sem.at[0],
-                matrix_sem.at[m], device_id={"row": peer}, device_id_type=MESH,
-            ).start()
-            return carry
-
-        lax.fori_loop(1, ROWS, send_block, 0)
+        lax.fori_loop(1 + (BATCH if m == 0 else 0), ROWS, functools.partial(send_block, m), 0)
         pltpu.make_async_copy(
-            masked.at[row * mu_per + m], matrix.at[m, n_rows], own_sem.at[m]
-        ).start()
-
-    slab, first = Z * nu_loc, SPLIT * nu_loc
+            masked.at[row * mu_per + m], matrix.at[m, z_rows(0)], own_sem.at[m]
+        ).start()
+
     sizes = (first, slab - first)
 
     def rows_of(g, dx):
         start = lax.rem(x + dx, X) * slab + g * first
         return pl.ds(pl.multiple_of(start, nu_loc), sizes[g])
-
-    def wait_rows(count, sem):
-        block = whole.at[0, pl.ds(0, count)]
-        pltpu.make_async_copy(block, block, sem).wait()
 
     def one(g, d):
         return (rows_of(0, d), col) if g == 0 else (rows_of(1, 0), col_at(d))
@@ -149,15 +174,19 @@
         wait_rows(sizes[g], relay_sem.at[g, i])
         send_coef(4, rows, which, core_sem, col=partner)
 
+    def begin(g):
+        rows, which = one(g, 0)
+        for s in (1, 3, 2):
+            send_coef(1, rows, which, x_sem.at[g, s - 1], **first_to(g, s))
+        spread(g, 0)
+
     order = (0, 3, 1, 2)
-    groups = [g for g in range(2) if sizes[g]]
-    wait_rows((Z - 1) * nu_loc, z_sem)
-    for s in (1, 3, 2):
-        for g in groups:
-            rows, which = one(g, 0)
-            send_coef(1, rows, which, x_sem.at[g, s - 1], **first_to(g, s))
-    for g in groups:
-        spread(g, 0)
+    groups = (0, 1)
+    for s in (1, -1):
+        wait_rows(nu_loc, z_sem.at[2 + s])
+    begin(0)
+    wait_rows((Z - SPLIT) * nu_loc, z_sem.at[5])
+    begin(1)
     for s in (1, 3, 2):
         for g in groups[::-1]:
             arrive_first(g, s)
@@ -172,7 +201,7 @@
 
     for m in range(mu_per):
         own = pltpu.make_async_copy(
-            masked.at[row * mu_per + m], matrix.at[m, n_rows], own_sem.at[m]
+            masked.at[row * mu_per + m], matrix.at[m, z_rows(0)], own_sem.at[m]
         )
         own.wait()
         most = matrix.at[m, pl.ds(0, (ROWS - 1) * nu_loc)]
@@ -247,7 +276,7 @@
             pltpu.VMEM((COLS, nu_all, aux_loc), jnp.bfloat16),
             pltpu.VMEM((mu_per, nu_all, aux_loc), jnp.bfloat16),
             dma((6,)), dma((mu_per,)), dma((2,)), dma((mu_per,)), dma(()),
-            dma((5,)), dma(()), dma((2, 3)), dma((2, 2, 4)), dma((2, 4)), dma(()),
+            dma((5,)), dma((6,)), dma((2, 3)), dma((2, 2, 4)), dma((2, 4)), dma(()),
         ],
         compiler_params=pltpu.CompilerParams(
             collective_id=0, has_side_effects=True, vmem_limit_bytes=40 * 1024 * 1024

time: 110 us -> 106 us (0.964)
  Pallas kernels: 108 us -> 104 us
    pallas_call x1, Pallas kernels: 108 us -> 104 us  [per_device(): pl.pallas_call(kernel, out_shape=jax.ShapeDtypeStruct(tensor.shape, jnp.b...]
where the time goes in v3:
time: 106 us
  Pallas kernels  104 us (98%)
  local copies, waits for them, and re-layouts  1.32 us (1%)
    pallas_call x1, Pallas kernels, per_device(): pl.pallas_call(kernel, out_shape=jax.ShapeDtypeStruct(tensor.shape, jnp.b...  104 us

profile of v3, /device:TPU:1, one launch (start us, length us, event | category | flops | bytes accessed | tf_op | source)
XLA Modules:
  0.0 105.6 jit_solution(10780830108128282100)
XLA Ops:
  0.0 104.2 %shard_map.37 = bf16[64,64,256]{2,1,0:T(8,128)(2,1)S(1)} custom-call(s32[1,4]{1,0:T(1,128)} %bitcast.1, bf16[64,64,256]{2,1,0:T(8,128)(2,1)} %tensor.1, bf16[64,256]{1,0:T(8,128)(2,1)} %coef.1), custom_call_target="tpu_custom_call" | custom-call | tf_op jit(solution)/shard_map/pallas_call | solution.py:262
  104.3 1.3 %copy.5 = bf16[64,64,256]{2,1,0:T(8,128)(2,1)} copy(bf16[64,64,256]{2,1,0:T(8,128)(2,1)S(1)} %shard_map.37) | data formatting | bytes 4194304

commit v4 on v3

--- a/solution.py
+++ b/solution.py
@@ -12,7 +12,7 @@
 ROWS, COLS = X * Z, Y * CORES
 NEAR = 2
 SPLIT = 2 * NEAR + 1
-BATCH = 12
+BATCH = 14
 
 
 def kernel(
@@ -114,9 +114,11 @@
         ).start()
         return carry
 
-    lax.fori_loop(1, 1 + BATCH, functools.partial(send_block, 0), 0)
+    lax.fori_loop(1, 1 + 10, functools.partial(send_block, 0), 0)
 
     for s, half in ((2, 0), (-2, 1)):
+        if s < 0:
+            lax.fori_loop(1 + 10, 1 + BATCH, functools.partial(send_block, 0), 0)
         wait_rows(nu_loc, z_sem.at[2 + s])
         d = s // 2
         send_rows(0, col, z_rows(-s), z_rows(-s - d), z_sem.at[5], row=at(0, d % Z))

time: 106 us -> 106 us (level)
  no operation moved by 1% of the time
where the time goes in v4:
time: 106 us
  Pallas kernels  104 us (98%)
  local copies, waits for them, and re-layouts  1.32 us (1%)
    pallas_call x1, Pallas kernels, per_device(): pl.pallas_call(kernel, out_shape=jax.ShapeDtypeStruct(tensor.shape, jnp.b...  104 us

profile of v4, /device:TPU:1, one launch (start us, length us, event | category | flops | bytes accessed | tf_op | source)
XLA Modules:
  0.0 105.6 jit_solution(11072371018959977059)
XLA Ops:
  0.0 104.3 %shard_map.37 = bf16[64,64,256]{2,1,0:T(8,128)(2,1)S(1)} custom-call(s32[1,4]{1,0:T(1,128)} %bitcast.1, bf16[64,64,256]{2,1,0:T(8,128)(2,1)} %tensor.1, bf16[64,256]{1,0:T(8,128)(2,1)} %coef.1), custom_call_target="tpu_custom_call" | custom-call | tf_op jit(solution)/shard_map/pallas_call | solution.py:264
  104.3 1.3 %copy.5 = bf16[64,64,256]{2,1,0:T(8,128)(2,1)} copy(bf16[64,64,256]{2,1,0:T(8,128)(2,1)S(1)} %shard_map.37) | data formatting | bytes 4194304
